TPU v7x, 32 devices: a whole 2x2x4 slice. The times are simulated.
32 devices in a mesh: scan: 8 (over z, x), bin: 4 (over y, core).
Axes of the slice: x: 2, y: 2, z: 4, core: 2. Of those that a mesh axis runs over, the one named last changes fastest.
Arguments:
- tile_blocks: bfloat16 [64, 16, 256, 256], P('scan', 'bin'), may hold values from -0.25 to 0.25
- tile_pattern: int32 [2, 64], P(None, 'scan'), may hold values from 0 to 63, as said below
- tile_count: int32 [8], P('scan'), may hold values from 1 to 8, as said below
- initial_map: float32 [16, 4, 4096], P('bin', None, 'scan')
- measured: float32 [16, 4, 16384], P('bin', None, 'scan')
- step_size: float32 [1], replicated, may hold values from 0.06 to 0.1
- penalty: float32 [4096], P('scan'), may hold values from 40 to 200
Outputs:
- source_map: float32 [16, 4, 4096], P('bin', None, 'scan')
Inputs may be any that keep to these rules, and one draw needn't show every extreme that they name: `tile_pattern`: row 0 names a sensor block of 64; row 1 of slot s names one of the 2 scan tiles (s // 8) * 2 to (s // 8) * 2 + 1. Only the first tile_count[d] slots of index d of scan are live; in every draw some indices have all 8 slots live.
All inputs are finite; a program needn't handle non-finite values.
Results may differ from a plain program's by a relative error of at most 0.00074.
Values may be sent and summed in bfloat16 or wider, within the bound.
No kernel may reach another device: no remote copies, remote signals or barrier semaphores. Data moves between devices by JAX's collectives and lax.ppermute only.
A program may use at most 64 MiB of HBM per device.

v0:
```python
import jax
import jax.numpy as jnp
from jax import lax
from jax.sharding import PartitionSpec as P

ITERS = 2


def add_forward(partial_value, tile_set, block_rows, block_cols, points, first_slot, end_slot):
    tile_width = tile_set.shape[-1]

    def advance(slot_id, running):
        matrix = lax.dynamic_index_in_dim(tile_set, slot_id, 0, keepdims=False)
        source = lax.dynamic_slice_in_dim(points, block_cols[slot_id] * tile_width, tile_width, 2)
        contrib = jnp.einsum("fij,fsj->fsi", matrix, source, preferred_element_type=jnp.float32)
        start = block_rows[slot_id] * tile_width
        present = lax.dynamic_slice_in_dim(running, start, tile_width, 2)
        return lax.dynamic_update_slice_in_dim(running, present + contrib, start, 2)

    return lax.fori_loop(first_slot, end_slot, advance, partial_value)


def add_backward(gradient, tile_set, block_rows, block_cols, residual, first_slot, end_slot):
    tile_width = tile_set.shape[-1]

    def advance(slot_id, running):
        matrix = lax.dynamic_index_in_dim(tile_set, slot_id, 0, keepdims=False)
        source = lax.dynamic_slice_in_dim(residual, block_rows[slot_id] * tile_width, tile_width, 2)
        contrib = jnp.einsum("fij,fsi->fsj", matrix, source, preferred_element_type=jnp.float32)
        start = block_cols[slot_id] * tile_width
        present = lax.dynamic_slice_in_dim(running, start, tile_width, 2)
        return lax.dynamic_update_slice_in_dim(running, present + contrib, start, 2)

    return lax.fori_loop(first_slot, end_slot, advance, gradient)


def home_slots(rows, tile_width, sensors_dev, homed):
    return rows * tile_width // sensors_dev * homed + rows % homed


def body(tile_blocks, tile_pattern, tile_count, initial_map, measured, step_size, penalty):
    tile_width = tile_blocks.shape[-1]
    per_device = initial_map.shape[2] // tile_width
    block_rows = tile_pattern[0]
    block_cols = tile_pattern[1] - lax.axis_index("scan") * per_device
    live_count = tile_count[0]
    bins_dev, snapshots, sensors_dev = measured.shape
    scan_count = lax.axis_size("scan")
    sensors = sensors_dev * scan_count
    homed = max(1, sensors_dev // tile_width)
    measured_all = lax.all_gather(measured, "scan", axis=2, tiled=True)
    block_rows = home_slots(block_rows, tile_width, sensors_dev, homed)
    own_measured = lax.dynamic_slice_in_dim(
        measured_all, lax.axis_index("scan") * sensors_dev, homed * tile_width, 2
    )
    sensors = scan_count * homed * tile_width
    current = initial_map
    for iteration in range(ITERS):
        rounded_map = current.astype(jnp.bfloat16)
        partial_value = jnp.zeros((bins_dev, snapshots, sensors), jnp.float32)
        partial_value = add_forward(
            partial_value, tile_blocks, block_rows, block_cols, rounded_map, 0, live_count
        )
        outgoing = partial_value.reshape(bins_dev, snapshots, scan_count, homed * tile_width)
        arrived = lax.all_to_all(outgoing, "scan", split_axis=2, concat_axis=2, tiled=True)
        totals = jnp.sum(arrived, axis=2)
        rounded = (totals - own_measured).astype(jnp.bfloat16)
        residual = lax.all_gather(rounded, "scan", axis=2, tiled=True)
        gradient = jnp.zeros_like(current)
        gradient = add_backward(
            gradient, tile_blocks, block_rows, block_cols, residual, 0, live_count
        )
        moved = current - step_size[0] * gradient
        energy = lax.psum(jnp.sum(moved * moved, axis=(0, 1)), "bin")
        current = moved * jnp.maximum(0.0, 1.0 - step_size[0] * penalty / jnp.sqrt(energy + 1e-06))
    return current


def solution(mesh):
    in_specs = (
        P("scan", "bin", None, None),
        P(None, "scan"),
        P("scan"),
        P("bin", None, "scan"),
        P("bin", None, "scan"),
        P(),
        P("scan"),
    )
    out_specs = P("bin", None, "scan")
    return jax.shard_map(body, mesh=mesh, in_specs=in_specs, out_specs=out_specs, check_vma=False)
```

profile of v0, /device:TPU:12, one launch (start us, length us, event | category | flops | bytes accessed | tf_op | source)
XLA Modules:
  0.0 327.0 jit_solution(14422891736312756115)
XLA Ops:
  8.8 38.3 %while.40 = (s32[]{:T(128)}, f32[4,4,16384]{2,1,0:T(4,128)S(1)}, s32[]{:T(128)}, s32[8]{0:T(128)S(1)}, s32[8]{0:T(128)S(1)}, /*index=5*/bf16[4,4,512]{2,1,0:T(4,...) while((s32[]{:T(128)}, f32[4,4,16384]{2,1,0:T(4,128)S(1)}, ...), condition=%wide.region_1.2_spmd, body=%wide.region_0.1_spmd.sunk | while | flops 2101261 | bytes 565535 | solution.py:20
  12.2 1.3 fusion.36
  16.9 1.3 fusion.36
  21.6 1.3 fusion.36
  26.4 1.3 fusion.36
  31.1 1.3 fusion.36
  35.8 1.3 fusion.36
  40.5 1.3 fusion.36
  45.2 1.3 fusion.36
  47.2 1.1 copy.15
  48.3 5.5 %all-to-all-start = ((f32[4,4,8,2048]{3,1,0,2:T(4,128)}), f32[4,4,8,2048]{3,1,0,2:T(4,128)S(1)}, u32[]{:S(2)}, u32[]{:S(2)}) async-start(f32[4,4,8,2048]{3,1,0,2:T(4,128)} %bitcast.36), calls=%async_computation | async-start | bytes 2097152 | tf_op jit(solution)/shard_map/all_to_all | solution.py:65
  55.1 26.2 %all-to-all-done = f32[4,4,8,2048]{3,1,0,2:T(4,128)S(1)} async-done(((f32[4,4,8,2048]{3,1,0,2:T(4,128)}), f32[4,4,8,2048]{3,1,0,2:T(4,128)S(1)}, u32[]{:S(2)}, u32[]{:S(2)}) %all-to-all-start) | async-done | bytes 1048608 | tf_op jit(solution)/shard_map/all_to_all | solution.py:65
  81.5 20.1 %all-gather.2.cloned.1.call-done = f32[4,4,16384]{2,1,0:T(4,128)} async-done(((f32[4,4,2048]{2,1,0:T(4,128)}), f32[4,4,16384]{2,1,0:T(4,128)}) %all-gather.2.cloned.1.call-update) | async-done | bytes 1048592 | tf_op jit(solution)/shard_map/all_gather | solution.py:51
  102.6 29.9 %all_gather.10 = bf16[4,4,16384]{2,1,0:T(4,128)(2,1)S(1)} all-gather(bf16[4,4,2048]{2,1,0:T(4,128)(2,1)S(1)} %subtract_convert_fusion.1), channel_id=1, replica_groups=mesh['scan'=8,'bin'=4] {'scan'}, dimensions={2}, use_global_device_ids=true | all-gather | bytes 589824 | tf_op jit(solution)/shard_map/all_gather | solution.py:68
  132.5 37.8 %while.41 = (s32[]{:T(128)}, f32[4,4,512]{2,1,0:T(4,128)S(1)}, s32[]{:T(128)}, s32[8]{0:T(128)S(1)}, s32[8]{0:T(128)S(1)}, /*index=5*/bf16[4,4,16384]{2,1,0:T(4,...) while((s32[]{:T(128)}, f32[4,4,512]{2,1,0:T(4,128)S(1)}, ...), condition=%wide.region_4.5_spmd, body=%wide.region_3.4_spmd.sunk | while | flops 2101261 | bytes 565535 | solution.py:34
  135.9 1.2 fusion.39
  140.5 1.2 fusion.39
  145.2 1.2 fusion.39
  149.8 1.2 fusion.39
  154.5 1.2 fusion.39
  159.1 1.2 fusion.39
  163.7 1.2 fusion.39
  168.4 1.2 fusion.39
  170.3 5.9 %psum.14 = f32[512]{0:T(512)S(1)} all-reduce(f32[512]{0:T(512)S(1)} %get-tuple-element.217), channel_id=1, replica_groups=mesh['scan'=8,'bin'=4] {'bin'}, use_global_device_ids=true, to_apply=%region_6.7 | all-reduce | flops 512 | bytes 4096 | tf_op jit(solution)/shard_map/psum | solution.py:74
  176.4 38.3 %while.42 = (s32[]{:T(128)}, f32[4,4,16384]{2,1,0:T(4,128)S(1)}, s32[]{:T(128)}, s32[8]{0:T(128)S(1)}, s32[8]{0:T(128)S(1)}, /*index=5*/bf16[4,4,512]{2,1,0:T(4,...) while((s32[]{:T(128)}, f32[4,4,16384]{2,1,0:T(4,128)S(1)}, ...), condition=%wide.region_8.9_spmd, body=%wide.region_7.8_spmd.sunk | while | flops 2101261 | bytes 565535 | solution.py:20
  179.8 1.3 fusion.42
  184.5 1.3 fusion.42
  189.2 1.3 fusion.42
  193.9 1.3 fusion.42
  198.6 1.3 fusion.42
  203.3 1.3 fusion.42
  208.0 1.3 fusion.42
  212.7 1.3 fusion.42
  214.7 1.1 copy.14
  215.8 5.1 %all-to-all-start.1 = ((f32[4,4,8,2048]{3,1,0,2:T(4,128)}), f32[4,4,8,2048]{3,1,0,2:T(4,128)S(1)}, u32[]{:S(2)}, u32[]{:S(2)}) async-start(f32[4,4,8,2048]{3,1,0,2:T(4,128)} %bitcast.35), calls=%async_computation.1 | async-start | bytes 2097152 | tf_op jit(solution)/shard_map/all_to_all | solution.py:65
  220.9 23.2 %all-to-all-done.1 = f32[4,4,8,2048]{3,1,0,2:T(4,128)S(1)} async-done(((f32[4,4,8,2048]{3,1,0,2:T(4,128)}), f32[4,4,8,2048]{3,1,0,2:T(4,128)S(1)}, u32[]{:S(2)}, u32[]{:S(2)}) %all-to-all-start.1) | async-done | bytes 1048608 | tf_op jit(solution)/shard_map/all_to_all | solution.py:65
  244.3 0.9 subtract_convert_fusion
  245.2 30.7 %all_gather.11 = bf16[4,4,16384]{2,1,0:T(4,128)(2,1)S(1)} all-gather(bf16[4,4,2048]{2,1,0:T(4,128)(2,1)S(1)} %subtract_convert_fusion), channel_id=1, replica_groups=mesh['scan'=8,'bin'=4] {'scan'}, dimensions={2}, use_global_device_ids=true | all-gather | bytes 589824 | tf_op jit(solution)/shard_map/all_gather | solution.py:68
  275.9 37.8 %while.43 = (s32[]{:T(128)}, f32[4,4,512]{2,1,0:T(4,128)S(1)}, s32[]{:T(128)}, s32[8]{0:T(128)S(1)}, s32[8]{0:T(128)S(1)}, /*index=5*/bf16[4,4,16384]{2,1,0:T(4,...) while((s32[]{:T(128)}, f32[4,4,512]{2,1,0:T(4,128)S(1)}, ...), condition=%wide.region_11.12_spmd, body=%wide.region_10.11_spmd.sunk | while | flops 2101261 | bytes 565535 | solution.py:34
  279.4 1.2 fusion.45
  284.0 1.2 fusion.45
  288.6 1.2 fusion.45
  293.3 1.2 fusion.45
  297.9 1.2 fusion.45
  302.6 1.2 fusion.45
  307.2 1.2 fusion.45
  311.9 1.2 fusion.45
  313.8 5.8 %psum.15 = f32[512]{0:T(512)S(1)} all-reduce(f32[512]{0:T(512)S(1)} %multiply_reduce_fusion), channel_id=1, replica_groups=mesh['scan'=8,'bin'=4] {'bin'}, use_global_device_ids=true, to_apply=%region_13.14 | all-reduce | flops 512 | bytes 4096 | tf_op jit(solution)/shard_map/psum | solution.py:74
  (86 shorter events, 47.9 us)
Async XLA Ops:
  48.3 122.0 %copy-start = (f32[4,4,512]{2,1,0:T(4,128)S(1)}, f32[4,4,512]{2,1,0:T(4,128)}, u32[]{:S(2)}) copy-start(f32[4,4,512]{2,1,0:T(4,128)} %param.18) | copy-start | bytes 98308
  48.3 127.9 %copy-start.1 = (f32[512]{0:T(512)S(1)}, f32[512]{0:T(512)}, u32[]{:S(2)}) copy-start(f32[512]{0:T(512)} %param.21) | copy-start | bytes 6148
  48.3 33.0 %all-to-all-start = ((f32[4,4,8,2048]{3,1,0,2:T(4,128)}), f32[4,4,8,2048]{3,1,0,2:T(4,128)S(1)}, u32[]{:S(2)}, u32[]{:S(2)}) async-start(f32[4,4,8,2048]{3,1,0,2:T(4,128)} %bitcast.36), calls=%async_computation | async-start | bytes 2097152 | tf_op jit(solution)/shard_map/all_to_all | solution.py:65
  53.7 47.9 %all-gather.2.cloned.1.call-start = ((), (), s32[]{:S(2)}) async-start(), calls=%async_computation.2 | async-start | bytes 1179648 | tf_op jit(solution)/shard_map/all_gather | solution.py:51
  215.8 28.3 %all-to-all-start.1 = ((f32[4,4,8,2048]{3,1,0,2:T(4,128)}), f32[4,4,8,2048]{3,1,0,2:T(4,128)S(1)}, u32[]{:S(2)}, u32[]{:S(2)}) async-start(f32[4,4,8,2048]{3,1,0,2:T(4,128)} %bitcast.35), calls=%async_computation.1 | async-start | bytes 2097152 | tf_op jit(solution)/shard_map/all_to_all | solution.py:65
Sparse Core Ops, SparseCore 0:
  56.7 44.8 all-gather.1
where the time goes:
time: 330 us; the launch traced here: 327 us
  blocking collectives  72.3 us (22%)
  waiting for transfers between devices  70.2 us (21%)
  loops' own time  69.3 us (21%)
  local copies, waits for them, and re-layouts  45.2 us (14%)
  matrix products  40.3 us (12%)
  between operations  14.1 us (4%)
  starting transfers between devices  10.5 us (3%)
  other arithmetic  5.18 us (2%)
    all_gather x2, blocking collectives, body(): residual = lax.all_gather(rounded, 'scan', axis=2, tiled=True)  60.6 us
    all_to_all x2, waiting for transfers between devices, body(): lax.all_to_all(outgoing, 'scan', split_axis=2, concat_axis=2, tiled=True)  49.4 us
    another operation x2, loops' own time, add_forward(): return lax.fori_loop(first_slot, end_slot, advance, partial_value)  34.7 us
    another operation x2, loops' own time, add_backward(): return lax.fori_loop(first_slot, end_slot, advance, gradient)  34.5 us
    dot_general x16, matrix products, advance(): jnp.einsum('fij,fsj->fsi', matrix, source, preferred_element_type=jnp.flo...  20.6 us
    all_gather x1, waiting for transfers between devices, body(): measured_all = lax.all_gather(measured, 'scan', axis=2, tiled=True)  20.1 us
    dot_general x16, matrix products, advance(): jnp.einsum('fij,fsi->fsj', matrix, source, preferred_element_type=jnp.flo...  19.7 us
    psum x2, blocking collectives, body(): energy = lax.psum(jnp.sum(moved * moved, axis=(0, 1)), 'bin')  11.7 us
  transfers between devices with their start and end apart: 3, of which 3 were waited for; matrix products, arithmetic and copies ran while one was open for 0% of the time, Pallas kernels for 0%

commit v1 on v0

--- a/solution.py
+++ b/solution.py
@@ -65,7 +65,17 @@
         arrived = lax.all_to_all(outgoing, "scan", split_axis=2, concat_axis=2, tiled=True)
         totals = jnp.sum(arrived, axis=2)
         rounded = (totals - own_measured).astype(jnp.bfloat16)
-        residual = lax.all_gather(rounded, "scan", axis=2, tiled=True)
+        n_lanes = lax.psum(1, "scan")
+        t1 = sorted(((to_i, (to_i + 1) % n_lanes) for to_i in range(n_lanes)))
+        v_next = rounded
+        ledger = [v_next]
+        for kk in [*range(1, n_lanes)]:
+            v_next = lax.ppermute(v_next, "scan", perm=t1)
+            ledger.insert(0, v_next)
+        part_next = jnp.concatenate(ledger, axis=2)
+        next_value = lax.axis_index("scan")
+        tall = next_value + 1
+        residual = jnp.roll(part_next, tall * rounded.shape[2], axis=2)
         gradient = jnp.zeros_like(current)
         gradient = add_backward(
             gradient, tile_blocks, block_rows, block_cols, residual, 0, live_count

time: 330 us -> 351 us (1.064)
  waiting for transfers between devices: 70.2 us -> 131 us
  blocking collectives: 72.3 us -> 40.6 us
  starting transfers between devices: 10.5 us -> 6.36 us
    ppermute x0 -> x14, waiting for transfers between devices: none -> 83.6 us  [body(): v_next = lax.ppermute(v_next, 'scan', perm=t1)]
    all_gather x2 -> x0, blocking collectives: 60.6 us -> none  [body(): residual = lax.all_gather(rounded, 'scan', axis=2, tiled=True)]
    all_to_all x0 -> x1, blocking collectives: none -> 28.9 us  [body(): lax.all_to_all(outgoing, 'scan', split_axis=2, concat_axis=2, tiled=True)]
    all_to_all x2 -> x1, waiting for transfers between devices: 49.4 us -> 26.8 us  [body(): lax.all_to_all(outgoing, 'scan', split_axis=2, concat_axis=2, tiled=True)]
    all_to_all x2 -> x1, starting transfers between devices: 10.5 us -> 5.45 us  [body(): lax.all_to_all(outgoing, 'scan', split_axis=2, concat_axis=2, tiled=True)]
  transfers between devices with their start and end apart: 3 -> 16, of which waited for: 3 -> 16; matrix products, arithmetic and copies ran while one was open for 0% -> 0% of each run, Pallas kernels for 0% -> 0%
where the time goes in v1:
time: 351 us; the launch traced here: 349 us
  waiting for transfers between devices  131 us (37%)
  loops' own time  66.2 us (19%)
  local copies, waits for them, and re-layouts  42.8 us (12%)
  blocking collectives  40.6 us (12%)
  matrix products  40.3 us (11%)
  between operations  14.2 us (4%)
  other arithmetic  6.82 us (2%)
  starting transfers between devices  6.36 us (2%)
    ppermute x14, waiting for transfers between devices, body(): v_next = lax.ppermute(v_next, 'scan', perm=t1)  83.6 us
    another operation x2, loops' own time, add_forward(): return lax.fori_loop(first_slot, end_slot, advance, partial_value)  33.2 us
    another operation x2, loops' own time, add_backward(): return lax.fori_loop(first_slot, end_slot, advance, gradient)  33 us
    all_to_all x1, blocking collectives, body(): lax.all_to_all(outgoing, 'scan', split_axis=2, concat_axis=2, tiled=True)  28.9 us
    all_to_all x1, waiting for transfers between devices, body(): lax.all_to_all(outgoing, 'scan', split_axis=2, concat_axis=2, tiled=True)  26.8 us
    dot_general x16, matrix products, advance(): jnp.einsum('fij,fsj->fsi', matrix, source, preferred_element_type=jnp.flo...  20.6 us
    all_gather x1, waiting for transfers between devices, body(): measured_all = lax.all_gather(measured, 'scan', axis=2, tiled=True)  20.1 us
    dot_general x16, matrix products, advance(): jnp.einsum('fij,fsi->fsj', matrix, source, preferred_element_type=jnp.flo...  19.7 us
  transfers between devices with their start and end apart: 16, of which 16 were waited for; matrix products, arithmetic and copies ran while one was open for 0% of the time, Pallas kernels for 0%

profile of v1, /device:TPU:12, one launch (start us, length us, event | category | flops | bytes accessed | tf_op | source)
XLA Modules:
  0.0 348.6 jit_solution(6441512450516368854)
XLA Ops:
  8.8 38.0 %while.40 = (s32[]{:T(128)}, f32[4,4,16384]{2,1,0:T(4,128)S(1)}, s32[]{:T(128)}, s32[8]{0:T(128)S(1)}, s32[8]{0:T(128)S(1)}, /*index=5*/bf16[4,4,512]{2,1,0:T(4,...) while((s32[]{:T(128)}, f32[4,4,16384]{2,1,0:T(4,128)S(1)}, ...), condition=%wide.region_1.2_spmd, body=%wide.region_0.1_spmd.sunk | while | flops 2101261 | bytes 565535 | solution.py:20
  12.2 1.3 fusion.38
  16.9 1.3 fusion.38
  21.5 1.3 fusion.38
  26.2 1.3 fusion.38
  30.9 1.3 fusion.38
  35.5 1.3 fusion.38
  40.2 1.3 fusion.38
  44.9 1.3 fusion.38
  48.0 5.5 %all-to-all-start = ((f32[4,4,8,2048]{3,1,0,2:T(4,128)}), f32[4,4,8,2048]{3,1,0,2:T(4,128)S(1)}, u32[]{:S(2)}, u32[]{:S(2)}) async-start(f32[4,4,8,2048]{3,1,0,2:T(4,128)} %bitcast.36), calls=%async_computation | async-start | bytes 2097152 | tf_op jit(solution)/shard_map/all_to_all | solution.py:65
  54.1 26.8 %all-to-all-done = f32[4,4,8,2048]{3,1,0,2:T(4,128)S(1)} async-done(((f32[4,4,8,2048]{3,1,0,2:T(4,128)}), f32[4,4,8,2048]{3,1,0,2:T(4,128)S(1)}, u32[]{:S(2)}, u32[]{:S(2)}) %all-to-all-start) | async-done | bytes 1048608 | tf_op jit(solution)/shard_map/all_to_all | solution.py:65
  81.2 20.1 %all-gather.2.cloned.1.call-done = f32[4,4,16384]{2,1,0:T(4,128)} async-done(((f32[4,4,2048]{2,1,0:T(4,128)}), f32[4,4,16384]{2,1,0:T(4,128)}) %all-gather.2.cloned.1.call-update) | async-done | bytes 1048592 | tf_op jit(solution)/shard_map/all_gather | solution.py:51
  102.9 4.6 %collective-permute-done = bf16[4,4,2048]{2,1,0:T(4,128)(2,1)S(1)} collective-permute-done((bf16[4,4,2048]{2,1,0:T(4,128)(2,1)S(1)}, bf16[4,4,2048]{2,1,0:T(4,128)(2,1)S(1)}, u32[]{:S(2)}, u32[]{:S(2)}) %collective-permute-start) | collective-permute-done | bytes 65568 | tf_op jit(solution)/shard_map/ppermute | solution.py:73
  107.5 5.2 %collective-permute-done.1 = bf16[4,4,2048]{2,1,0:T(4,128)(2,1)S(1)} collective-permute-done((bf16[4,4,2048]{2,1,0:T(4,128)(2,1)S(1)}, bf16[4,4,2048]{2,1,0:T(4,128)(2,1)S(1)}, u32[]{:S(2)}, u32[]{:S(2)}) %collective-permute-start.1) | collective-permute-done | bytes 65568 | tf_op jit(solution)/shard_map/ppermute | solution.py:73
  112.7 5.5 %collective-permute-done.2 = bf16[4,4,2048]{2,1,0:T(4,128)(2,1)S(1)} collective-permute-done((bf16[4,4,2048]{2,1,0:T(4,128)(2,1)S(1)}, bf16[4,4,2048]{2,1,0:T(4,128)(2,1)S(1)}, u32[]{:S(2)}, u32[]{:S(2)}) %collective-permute-start.2) | collective-permute-done | bytes 65568 | tf_op jit(solution)/shard_map/ppermute | solution.py:73
  118.2 6.3 %collective-permute-done.3 = bf16[4,4,2048]{2,1,0:T(4,128)(2,1)S(1)} collective-permute-done((bf16[4,4,2048]{2,1,0:T(4,128)(2,1)S(1)}, bf16[4,4,2048]{2,1,0:T(4,128)(2,1)S(1)}, u32[]{:S(2)}, u32[]{:S(2)}) %collective-permute-start.3) | collective-permute-done | bytes 65568 | tf_op jit(solution)/shard_map/ppermute | solution.py:73
  124.5 6.9 %collective-permute-done.4 = bf16[4,4,2048]{2,1,0:T(4,128)(2,1)S(1)} collective-permute-done((bf16[4,4,2048]{2,1,0:T(4,128)(2,1)S(1)}, bf16[4,4,2048]{2,1,0:T(4,128)(2,1)S(1)}, u32[]{:S(2)}, u32[]{:S(2)}) %collective-permute-start.4) | collective-permute-done | bytes 65568 | tf_op jit(solution)/shard_map/ppermute | solution.py:73
  131.4 6.7 %collective-permute-done.5 = bf16[4,4,2048]{2,1,0:T(4,128)(2,1)S(1)} collective-permute-done((bf16[4,4,2048]{2,1,0:T(4,128)(2,1)S(1)}, bf16[4,4,2048]{2,1,0:T(4,128)(2,1)S(1)}, u32[]{:S(2)}, u32[]{:S(2)}) %collective-permute-start.5) | collective-permute-done | bytes 65568 | tf_op jit(solution)/shard_map/ppermute | solution.py:73
  138.7 6.3 %collective-permute-done.6 = bf16[4,4,2048]{2,1,0:T(4,128)(2,1)S(1)} collective-permute-done((bf16[4,4,2048]{2,1,0:T(4,128)(2,1)S(1)}, bf16[4,4,2048]{2,1,0:T(4,128)(2,1)S(1)}, u32[]{:S(2)}, u32[]{:S(2)}) %collective-permute-start.6) | collective-permute-done | bytes 65568 | tf_op jit(solution)/shard_map/ppermute | solution.py:73
  146.2 35.6 %while.41 = (s32[]{:T(128)}, f32[4,4,512]{2,1,0:T(4,128)S(1)}, s32[]{:T(128)}, s32[8]{0:T(128)S(1)}, s32[8]{0:T(128)S(1)}, /*index=5*/bf16[4,4,16384]{2,1,0:T(4,...) while((s32[]{:T(128)}, f32[4,4,512]{2,1,0:T(4,128)S(1)}, ...), condition=%wide.region_4.6_spmd, body=%wide.region_3.5_spmd.sunk | while | flops 2101261 | bytes 565535 | solution.py:34
  149.3 1.2 fusion.41
  153.7 1.2 fusion.41
  158.0 1.2 fusion.41
  162.4 1.2 fusion.41
  171.1 1.2 fusion.41
  175.5 1.2 fusion.41
  179.9 1.2 fusion.41
  181.8 5.9 %psum.14 = f32[512]{0:T(512)S(1)} all-reduce(f32[512]{0:T(512)S(1)} %get-tuple-element.218), channel_id=1, replica_groups=mesh['scan'=8,'bin'=4] {'bin'}, use_global_device_ids=true, to_apply=%region_6.8 | all-reduce | flops 512 | bytes 4096 | tf_op jit(solution)/shard_map/psum | solution.py:84
  187.9 36.1 %while.42 = (s32[]{:T(128)}, f32[4,4,16384]{2,1,0:T(4,128)S(1)}, s32[]{:T(128)}, s32[8]{0:T(128)S(1)}, s32[8]{0:T(128)S(1)}, /*index=5*/bf16[4,4,512]{2,1,0:T(4,...) while((s32[]{:T(128)}, f32[4,4,16384]{2,1,0:T(4,128)S(1)}, ...), condition=%wide.region_8.10_spmd, body=%wide.region_7.9_spmd.sunk | while | flops 2101261 | bytes 565535 | solution.py:20
  191.0 1.3 fusion.44
  195.5 1.3 fusion.44
  199.9 1.3 fusion.44
  204.3 1.3 fusion.44
  208.8 1.3 fusion.44
  213.2 1.3 fusion.44
  217.7 1.3 fusion.44
  222.1 1.3 fusion.44
  224.2 28.9 %all_to_all.10 = f32[4,4,8,2048]{3,1,0,2:T(4,128)S(1)} all-to-all(f32[4,4,8,2048]{3,1,0,2:T(4,128)S(1)} %bitcast.68), channel_id=1, replica_groups=mesh['scan'=8,'bin'=4] {'scan'}, dimensions={2} | all-to-all | bytes 2097152 | tf_op jit(solution)/shard_map/all_to_all | solution.py:65
  254.5 5.0 %collective-permute-done.7 = bf16[4,4,2048]{2,1,0:T(4,128)(2,1)S(1)} collective-permute-done((bf16[4,4,2048]{2,1,0:T(4,128)(2,1)S(1)}, bf16[4,4,2048]{2,1,0:T(4,128)(2,1)S(1)}, u32[]{:S(2)}, u32[]{:S(2)}) %collective-permute-start.7) | collective-permute-done | bytes 65568 | tf_op jit(solution)/shard_map/ppermute | solution.py:73
  259.4 5.8 %collective-permute-done.8 = bf16[4,4,2048]{2,1,0:T(4,128)(2,1)S(1)} collective-permute-done((bf16[4,4,2048]{2,1,0:T(4,128)(2,1)S(1)}, bf16[4,4,2048]{2,1,0:T(4,128)(2,1)S(1)}, u32[]{:S(2)}, u32[]{:S(2)}) %collective-permute-start.8) | collective-permute-done | bytes 65568 | tf_op jit(solution)/shard_map/ppermute | solution.py:73
  265.2 5.4 %collective-permute-done.9 = bf16[4,4,2048]{2,1,0:T(4,128)(2,1)S(1)} collective-permute-done((bf16[4,4,2048]{2,1,0:T(4,128)(2,1)S(1)}, bf16[4,4,2048]{2,1,0:T(4,128)(2,1)S(1)}, u32[]{:S(2)}, u32[]{:S(2)}) %collective-permute-start.9) | collective-permute-done | bytes 65568 | tf_op jit(solution)/shard_map/ppermute | solution.py:73
  270.6 5.8 %collective-permute-done.10 = bf16[4,4,2048]{2,1,0:T(4,128)(2,1)S(1)} collective-permute-done((bf16[4,4,2048]{2,1,0:T(4,128)(2,1)S(1)}, bf16[4,4,2048]{2,1,0:T(4,128)(2,1)S(1)}, u32[]{:S(2)}, u32[]{:S(2)}) %collective-permute-start.10) | collective-permute-done | bytes 65568 | tf_op jit(solution)/shard_map/ppermute | solution.py:73
  276.4 6.2 %collective-permute-done.11 = bf16[4,4,2048]{2,1,0:T(4,128)(2,1)S(1)} collective-permute-done((bf16[4,4,2048]{2,1,0:T(4,128)(2,1)S(1)}, bf16[4,4,2048]{2,1,0:T(4,128)(2,1)S(1)}, u32[]{:S(2)}, u32[]{:S(2)}) %collective-permute-start.11) | collective-permute-done | bytes 65568 | tf_op jit(solution)/shard_map/ppermute | solution.py:73
  282.6 7.2 %collective-permute-done.12 = bf16[4,4,2048]{2,1,0:T(4,128)(2,1)S(1)} collective-permute-done((bf16[4,4,2048]{2,1,0:T(4,128)(2,1)S(1)}, bf16[4,4,2048]{2,1,0:T(4,128)(2,1)S(1)}, u32[]{:S(2)}, u32[]{:S(2)}) %collective-permute-start.12) | collective-permute-done | bytes 65568 | tf_op jit(solution)/shard_map/ppermute | solution.py:73
  289.8 6.8 %collective-permute-done.13 = bf16[4,4,2048]{2,1,0:T(4,128)(2,1)S(1)} collective-permute-done((bf16[4,4,2048]{2,1,0:T(4,128)(2,1)S(1)}, bf16[4,4,2048]{2,1,0:T(4,128)(2,1)S(1)}, u32[]{:S(2)}, u32[]{:S(2)}) %collective-permute-start.13) | collective-permute-done | bytes 65568 | tf_op jit(solution)/shard_map/ppermute | solution.py:73
  297.8 37.5 %while.43 = (s32[]{:T(128)}, f32[4,4,512]{2,1,0:T(4,128)S(1)}, s32[]{:T(128)}, s32[8]{0:T(128)S(1)}, s32[8]{0:T(128)S(1)}, /*index=5*/bf16[4,4,16384]{2,1,0:T(4,...) while((s32[]{:T(128)}, f32[4,4,512]{2,1,0:T(4,128)S(1)}, ...), condition=%wide.region_11.13_spmd, body=%wide.region_10.12_spmd.sunk | while | flops 2101261 | bytes 565535 | solution.py:34
  301.1 1.2 fusion.47
  335.3 5.9 %psum.15 = f32[512]{0:T(512)S(1)} all-reduce(f32[512]{0:T(512)S(1)} %multiply_reduce_fusion), channel_id=1, replica_groups=mesh['scan'=8,'bin'=4] {'bin'}, use_global_device_ids=true, to_apply=%region_13.15 | all-reduce | flops 512 | bytes 4096 | tf_op jit(solution)/shard_map/psum | solution.py:84
  (129 shorter events, 61.1 us)
Async XLA Ops:
  48.0 133.8 %copy-start = (f32[4,4,512]{2,1,0:T(4,128)S(1)}, f32[4,4,512]{2,1,0:T(4,128)}, u32[]{:S(2)}) copy-start(f32[4,4,512]{2,1,0:T(4,128)} %param.20) | copy-start | bytes 98308
  48.0 139.8 %copy-start.1 = (f32[512]{0:T(512)S(1)}, f32[512]{0:T(512)}, u32[]{:S(2)}) copy-start(f32[512]{0:T(512)} %param.23) | copy-start | bytes 6148
  48.0 33.0 %all-to-all-start = ((f32[4,4,8,2048]{3,1,0,2:T(4,128)}), f32[4,4,8,2048]{3,1,0,2:T(4,128)S(1)}, u32[]{:S(2)}, u32[]{:S(2)}) async-start(f32[4,4,8,2048]{3,1,0,2:T(4,128)} %bitcast.36), calls=%async_computation | async-start | bytes 2097152 | tf_op jit(solution)/shard_map/all_to_all | solution.py:65
  53.4 47.9 %all-gather.2.cloned.1.call-start = ((), (), s32[]{:S(2)}) async-start(), calls=%async_computation.2 | async-start | bytes 1179648 | tf_op jit(solution)/shard_map/all_gather | solution.py:51
  102.3 5.2 %collective-permute-start = (bf16[4,4,2048]{2,1,0:T(4,128)(2,1)S(1)}, bf16[4,4,2048]{2,1,0:T(4,128)(2,1)S(1)}, u32[]{:S(2)}, u32[]{:S(2)}) collective-permute-start(bf16[4,4,2048]{2,1,0:T(4,128)(2,1)S(1)} %subtract_convert_fusion.1), channel_id=1, source_target_pairs={{0,4},{4,8},{8,12},{12,16},{16,20},{20,24},{24,28},{28,0},{1,5},{5... | collective-permute-start | bytes 196616 | tf_op jit(solution)/shard_map/ppermute | solution.py:73
  107.5 5.2 %collective-permute-start.1 = (bf16[4,4,2048]{2,1,0:T(4,128)(2,1)S(1)}, bf16[4,4,2048]{2,1,0:T(4,128)(2,1)S(1)}, u32[]{:S(2)}, u32[]{:S(2)}) collective-permute-start(bf16[4,4,2048]{2,1,0:T(4,128)(2,1)S(1)} %collective-permute-done), channel_id=1, source_target_pairs={{0,4},{4,8},{8,12},{12,16},{16,20},{20,24},{24,28},{28,0},{1,5},{5... | collective-permute-start | bytes 196616 | tf_op jit(solution)/shard_map/ppermute | solution.py:73
  112.7 5.5 %collective-permute-start.2 = (bf16[4,4,2048]{2,1,0:T(4,128)(2,1)S(1)}, bf16[4,4,2048]{2,1,0:T(4,128)(2,1)S(1)}, u32[]{:S(2)}, u32[]{:S(2)}) collective-permute-start(bf16[4,4,2048]{2,1,0:T(4,128)(2,1)S(1)} %collective-permute-done.1), channel_id=1, source_target_pairs={{0,4},{4,8},{8,12},{12,16},{16,20},{20,24},{24,28},{28,0},{1,5},{5... | collective-permute-start | bytes 196616 | tf_op jit(solution)/shard_map/ppermute | solution.py:73
  118.2 6.3 %collective-permute-start.3 = (bf16[4,4,2048]{2,1,0:T(4,128)(2,1)S(1)}, bf16[4,4,2048]{2,1,0:T(4,128)(2,1)S(1)}, u32[]{:S(2)}, u32[]{:S(2)}) collective-permute-start(bf16[4,4,2048]{2,1,0:T(4,128)(2,1)S(1)} %collective-permute-done.2), channel_id=1, source_target_pairs={{0,4},{4,8},{8,12},{12,16},{16,20},{20,24},{24,28},{28,0},{1,5},{5... | collective-permute-start | bytes 196616 | tf_op jit(solution)/shard_map/ppermute | solution.py:73
  124.5 6.9 %collective-permute-start.4 = (bf16[4,4,2048]{2,1,0:T(4,128)(2,1)S(1)}, bf16[4,4,2048]{2,1,0:T(4,128)(2,1)S(1)}, u32[]{:S(2)}, u32[]{:S(2)}) collective-permute-start(bf16[4,4,2048]{2,1,0:T(4,128)(2,1)S(1)} %collective-permute-done.3), channel_id=1, source_target_pairs={{0,4},{4,8},{8,12},{12,16},{16,20},{20,24},{24,28},{28,0},{1,5},{5... | collective-permute-start | bytes 196616 | tf_op jit(solution)/shard_map/ppermute | solution.py:73
  131.4 6.7 %collective-permute-start.5 = (bf16[4,4,2048]{2,1,0:T(4,128)(2,1)S(1)}, bf16[4,4,2048]{2,1,0:T(4,128)(2,1)S(1)}, u32[]{:S(2)}, u32[]{:S(2)}) collective-permute-start(bf16[4,4,2048]{2,1,0:T(4,128)(2,1)S(1)} %collective-permute-done.4), channel_id=1, source_target_pairs={{0,4},{4,8},{8,12},{12,16},{16,20},{20,24},{24,28},{28,0},{1,5},{5... | collective-permute-start | bytes 196616 | tf_op jit(solution)/shard_map/ppermute | solution.py:73
  138.1 7.0 %collective-permute-start.6 = (bf16[4,4,2048]{2,1,0:T(4,128)(2,1)S(1)}, bf16[4,4,2048]{2,1,0:T(4,128)(2,1)S(1)}, u32[]{:S(2)}, u32[]{:S(2)}) collective-permute-start(bf16[4,4,2048]{2,1,0:T(4,128)(2,1)S(1)} %collective-permute-done.5), channel_id=1, source_target_pairs={{0,4},{4,8},{8,12},{12,16},{16,20},{20,24},{24,28},{28,0},{1,5},{5... | collective-permute-start | bytes 196616 | tf_op jit(solution)/shard_map/ppermute | solution.py:73
  254.2 5.2 %collective-permute-start.7 = (bf16[4,4,2048]{2,1,0:T(4,128)(2,1)S(1)}, bf16[4,4,2048]{2,1,0:T(4,128)(2,1)S(1)}, u32[]{:S(2)}, u32[]{:S(2)}) collective-permute-start(bf16[4,4,2048]{2,1,0:T(4,128)(2,1)S(1)} %subtract_convert_fusion), channel_id=1, source_target_pairs={{0,4},{4,8},{8,12},{12,16},{16,20},{20,24},{24,28},{28,0},{1,5},{5... | collective-permute-start | bytes 196616 | tf_op jit(solution)/shard_map/ppermute | solution.py:73
  259.4 5.8 %collective-permute-start.8 = (bf16[4,4,2048]{2,1,0:T(4,128)(2,1)S(1)}, bf16[4,4,2048]{2,1,0:T(4,128)(2,1)S(1)}, u32[]{:S(2)}, u32[]{:S(2)}) collective-permute-start(bf16[4,4,2048]{2,1,0:T(4,128)(2,1)S(1)} %collective-permute-done.7), channel_id=1, source_target_pairs={{0,4},{4,8},{8,12},{12,16},{16,20},{20,24},{24,28},{28,0},{1,5},{5... | collective-permute-start | bytes 196616 | tf_op jit(solution)/shard_map/ppermute | solution.py:73
  265.2 5.4 %collective-permute-start.9 = (bf16[4,4,2048]{2,1,0:T(4,128)(2,1)S(1)}, bf16[4,4,2048]{2,1,0:T(4,128)(2,1)S(1)}, u32[]{:S(2)}, u32[]{:S(2)}) collective-permute-start(bf16[4,4,2048]{2,1,0:T(4,128)(2,1)S(1)} %collective-permute-done.8), channel_id=1, source_target_pairs={{0,4},{4,8},{8,12},{12,16},{16,20},{20,24},{24,28},{28,0},{1,5},{5... | collective-permute-start | bytes 196616 | tf_op jit(solution)/shard_map/ppermute | solution.py:73
  270.6 5.8 %collective-permute-start.10 = (bf16[4,4,2048]{2,1,0:T(4,128)(2,1)S(1)}, bf16[4,4,2048]{2,1,0:T(4,128)(2,1)S(1)}, u32[]{:S(2)}, u32[]{:S(2)}) collective-permute-start(bf16[4,4,2048]{2,1,0:T(4,128)(2,1)S(1)} %collective-permute-done.9), channel_id=1, source_target_pairs={{0,4},{4,8},{8,12},{12,16},{16,20},{20,24},{24,28},{28,0},{1,5},{5... | collective-permute-start | bytes 196616 | tf_op jit(solution)/shard_map/ppermute | solution.py:73
  276.4 6.2 %collective-permute-start.11 = (bf16[4,4,2048]{2,1,0:T(4,128)(2,1)S(1)}, bf16[4,4,2048]{2,1,0:T(4,128)(2,1)S(1)}, u32[]{:S(2)}, u32[]{:S(2)}) collective-permute-start(bf16[4,4,2048]{2,1,0:T(4,128)(2,1)S(1)} %collective-permute-done.10), channel_id=1, source_target_pairs={{0,4},{4,8},{8,12},{12,16},{16,20},{20,24},{24,28},{28,0},{1,5},{5... | collective-permute-start | bytes 196616 | tf_op jit(solution)/shard_map/ppermute | solution.py:73
  282.6 7.2 %collective-permute-start.12 = (bf16[4,4,2048]{2,1,0:T(4,128)(2,1)S(1)}, bf16[4,4,2048]{2,1,0:T(4,128)(2,1)S(1)}, u32[]{:S(2)}, u32[]{:S(2)}) collective-permute-start(bf16[4,4,2048]{2,1,0:T(4,128)(2,1)S(1)} %collective-permute-done.11), channel_id=1, source_target_pairs={{0,4},{4,8},{8,12},{12,16},{16,20},{20,24},{24,28},{28,0},{1,5},{5... | collective-permute-start | bytes 196616 | tf_op jit(solution)/shard_map/ppermute | solution.py:73
  289.8 6.8 %collective-permute-start.13 = (bf16[4,4,2048]{2,1,0:T(4,128)(2,1)S(1)}, bf16[4,4,2048]{2,1,0:T(4,128)(2,1)S(1)}, u32[]{:S(2)}, u32[]{:S(2)}) collective-permute-start(bf16[4,4,2048]{2,1,0:T(4,128)(2,1)S(1)} %collective-permute-done.12), channel_id=1, source_target_pairs={{0,4},{4,8},{8,12},{12,16},{16,20},{20,24},{24,28},{28,0},{1,5},{5... | collective-permute-start | bytes 196616 | tf_op jit(solution)/shard_map/ppermute | solution.py:73
Sparse Core Ops, SparseCore 0:
  56.4 44.8 all-gather.1
